TPU v7x, 32 devices: a whole 2x2x4 slice. The times are simulated.
32 devices in a mesh: fsdp: 4 (over x, core), ctx: 4 (over z), tensor: 2 (over y).
Axes of the slice: x: 2, y: 2, z: 4, core: 2. Of those that a mesh axis runs over, the one named last changes fastest.
Arguments:
- block_input: bfloat16 [4096, 2048], P(('fsdp', 'ctx')), may hold values from -6 to 6
- seq_lengths: int32 [4, 3], P('fsdp'), may hold values from 1 to 512, 1024 in all within a row
- attn_gain: bfloat16 [2048], P('fsdp'), may hold values from 0.5 to 1.5
- w_query: bfloat16 [2048, 2048], P('fsdp', 'tensor'), as said below
- w_key: bfloat16 [2048, 512], P('fsdp', 'tensor'), as said below
- w_value: bfloat16 [2048, 512], P('fsdp', 'tensor'), may hold values from -0.125 to 0.125
- w_output: bfloat16 [2048, 2048], P('tensor', 'fsdp'), may hold values from -2 to 2
- mlp_gain: bfloat16 [2048], P('fsdp'), may hold values from 0.5 to 1.5
- w_gate: bfloat16 [2048, 8192], P('fsdp', 'tensor'), may hold values from -0.125 to 0.125
- w_up: bfloat16 [2048, 8192], P('fsdp', 'tensor'), may hold values from -0.125 to 0.125
- w_down: bfloat16 [8192, 2048], P('tensor', 'fsdp'), may hold values from -0.0625 to 0.0625
- cotangent: bfloat16 [4096, 2048], P(('fsdp', 'ctx')), may hold values from -6 to 6
Outputs:
- block_output: bfloat16 [4096, 2048], P(('fsdp', 'ctx'))
- input_grad: float32 [4096, 2048], P(('fsdp', 'ctx'))
- attn_gain_grad: float32 [2048], P('fsdp')
- query_grad: float32 [2048, 2048], P('fsdp', 'tensor')
- key_grad: float32 [2048, 512], P('fsdp', 'tensor')
- value_grad: float32 [2048, 512], P('fsdp', 'tensor')
- output_grad: float32 [2048, 2048], P('tensor', 'fsdp')
- mlp_gain_grad: float32 [2048], P('fsdp')
- gate_grad: float32 [2048, 8192], P('fsdp', 'tensor')
- up_grad: float32 [2048, 8192], P('fsdp', 'tensor')
- down_grad: float32 [8192, 2048], P('tensor', 'fsdp')
Inputs may be any that keep to these rules, and one draw needn't show every extreme that they name: `seq_lengths`: each row sums to 1024, and its largest entry is exactly 512. `w_query`: a projection matrix. `w_key`: a projection matrix.
All inputs are finite; a program needn't handle non-finite values.
Results may differ from a plain program's by a relative error of at most 0.02.
Values may be sent and summed in bfloat16 or wider, within the bound.
No kernel may reach another device: no remote copies, remote signals or barrier semaphores. Data moves between devices by JAX's collectives and lax.ppermute only.
A program may use at most 320 MiB of HBM per device.

v0:
```python
import math
import jax
import jax.numpy as jnp
from jax import lax
from jax.sharding import PartitionSpec as P

HD = 64
eps_norm = 1e-05
rope_base = 500000.0


def layout(lengths_row, token_index):
    seq_ends = jnp.cumsum(lengths_row)
    passed = (token_index[:, None] >= seq_ends[None, :]).astype(jnp.int32)
    segment = jnp.sum(passed, axis=1)
    seq_start = jnp.sum(passed * lengths_row[None, :], axis=1)
    return (segment, token_index - seq_start)


def rope_tables(position):
    half_width = HD // 2
    frequency = rope_base ** (-jnp.arange(half_width, dtype=jnp.float32) / half_width)
    angles = position.astype(jnp.float32)[:, None] * frequency[None, :]
    return (jnp.cos(angles), jnp.sin(angles))


def rotate(vectors, cosine_table, sine_table, direction):
    half_width = HD // 2
    first_half = vectors[..., :half_width]
    second = vectors[..., half_width:]
    cos_rows = cosine_table[:, None, :]
    sin_rows = direction * sine_table[:, None, :]
    return jnp.concatenate(
        [first_half * cos_rows - second * sin_rows, second * cos_rows + first_half * sin_rows],
        axis=-1,
    )


def norm_forward(rows_wide):
    inv_rms = lax.rsqrt(jnp.mean(rows_wide * rows_wide, axis=-1, keepdims=True) + eps_norm)
    return (rows_wide * inv_rms, inv_rms)


def norm_backward(delta_rows, unit_rows, inv_rms, gain_weights):
    scaled = gain_weights.astype(jnp.float32)[None, :] * delta_rows
    gain_term = jnp.sum(delta_rows * unit_rows, axis=0)
    back_term = inv_rms * (
        scaled - unit_rows * jnp.mean(scaled * unit_rows, axis=-1, keepdims=True)
    )
    return (gain_term, back_term)


def head_forward(queries, key_rows, values, allowed, score_scale):
    scores = (
        jnp.einsum("tgd,sd->gts", queries, key_rows, preferred_element_type=jnp.float32)
        * score_scale
    )
    masked = jnp.where(allowed[None], scores, -1e30)
    row_max = jnp.max(masked, axis=-1, keepdims=True)
    exp_total = jnp.sum(
        jnp.where(allowed[None], jnp.exp(masked - row_max), 0.0), axis=-1, keepdims=True
    )
    log_total = row_max + jnp.log(exp_total)
    attn_prob = jnp.where(allowed[None], jnp.exp(scores - log_total), 0.0).astype(jnp.bfloat16)
    attended = jnp.einsum(
        "gts,sd->tgd", attn_prob, values, preferred_element_type=jnp.float32
    ).astype(jnp.bfloat16)
    return (attended, log_total[..., 0])


def head_backward(
    queries, key_rows, values, log_total, out_delta, inner_rows, allowed, score_scale
):
    scores = (
        jnp.einsum("tgd,sd->gts", queries, key_rows, preferred_element_type=jnp.float32)
        * score_scale
    )
    attn_prob = jnp.where(allowed[None], jnp.exp(scores - log_total[..., None]), 0.0)
    prob_delta = jnp.einsum("tgd,sd->gts", out_delta, values, preferred_element_type=jnp.float32)
    score_delta = (attn_prob * (prob_delta - inner_rows[..., None]) * score_scale).astype(
        jnp.bfloat16
    )
    query_back = jnp.einsum(
        "gts,sd->tgd", score_delta, key_rows, preferred_element_type=jnp.float32
    )
    key_back = jnp.einsum("gts,tgd->sd", score_delta, queries, preferred_element_type=jnp.float32)
    value_back = jnp.einsum(
        "gts,tgd->sd", attn_prob.astype(jnp.bfloat16), out_delta, preferred_element_type=jnp.float32
    )
    return (query_back, key_back, value_back)


def body(
    block_input,
    seq_lengths,
    attn_gain,
    w_query,
    w_key,
    w_value,
    w_output,
    mlp_gain,
    w_gate,
    w_up,
    w_down,
    cotangent,
):
    row_count = block_input.shape[0]
    group_rows = row_count * lax.axis_size("ctx")
    lengths_row = seq_lengths[0]
    score_scale = 1.0 / math.sqrt(HD)
    gain_one, query_full, key_full, value_full, output_full = (
        lax.all_gather(attn_gain, "fsdp", axis=0, tiled=True),
        lax.all_gather(w_query, "fsdp", axis=0, tiled=True),
        lax.all_gather(w_key, "fsdp", axis=0, tiled=True),
        lax.all_gather(w_value, "fsdp", axis=0, tiled=True),
        lax.all_gather(w_output, "fsdp", axis=1, tiled=True),
    )
    heads_local = query_full.shape[1] // HD
    kv_local = key_full.shape[1] // HD
    head_share = heads_local // kv_local
    local_index = lax.axis_index("ctx") * row_count + jnp.arange(row_count, dtype=jnp.int32)
    group_index = jnp.arange(group_rows, dtype=jnp.int32)
    query_segment, query_position = layout(lengths_row, local_index)
    key_segment, key_position = layout(lengths_row, group_index)
    allowed = (query_segment[:, None] == key_segment[None, :]) & (
        group_index[None, :] <= local_index[:, None]
    )
    cosine_table, sine_table = rope_tables(query_position)
    input_wide = block_input.astype(jnp.float32)
    unit_one, rstd_one = norm_forward(input_wide)
    normed_one = (unit_one * gain_one.astype(jnp.float32)[None, :]).astype(jnp.bfloat16)
    query_pre = jnp.dot(normed_one, query_full, preferred_element_type=jnp.float32).reshape(
        row_count, heads_local, HD
    )
    key_pre = jnp.dot(normed_one, key_full, preferred_element_type=jnp.float32).reshape(
        row_count, kv_local, HD
    )
    value_rows = jnp.dot(normed_one, value_full, preferred_element_type=jnp.float32).astype(
        jnp.bfloat16
    )
    query_rot = rotate(query_pre, cosine_table, sine_table, 1.0).astype(jnp.bfloat16)
    key_rot = rotate(key_pre, cosine_table, sine_table, 1.0).astype(jnp.bfloat16)
    key_all, value_all = (
        lax.all_gather(key_rot.reshape(row_count, kv_local * HD), "ctx", axis=0, tiled=True),
        lax.all_gather(value_rows, "ctx", axis=0, tiled=True),
    )
    query_heads = jnp.moveaxis(query_rot.reshape(row_count, kv_local, head_share, HD), 1, 0)
    key_heads = jnp.moveaxis(key_all.reshape(group_rows, kv_local, HD), 1, 0)
    value_heads = jnp.moveaxis(value_all.reshape(group_rows, kv_local, HD), 1, 0)
    attended, log_total = lax.map(
        lambda parts_h: head_forward(parts_h[0], parts_h[1], parts_h[2], allowed, score_scale),
        (query_heads, key_heads, value_heads),
    )
    attended_rows = jnp.moveaxis(attended, 0, 1).reshape(row_count, heads_local * HD)
    attn_part = jnp.dot(attended_rows, output_full, preferred_element_type=jnp.float32)
    residual = input_wide + lax.psum(attn_part, "tensor")
    gain_two, gate_full, up_full, down_full = (
        lax.all_gather(mlp_gain, "fsdp", axis=0, tiled=True),
        lax.all_gather(w_gate, "fsdp", axis=0, tiled=True),
        lax.all_gather(w_up, "fsdp", axis=0, tiled=True),
        lax.all_gather(w_down, "fsdp", axis=1, tiled=True),
    )
    unit_two, rstd_two = norm_forward(residual)
    normed_two = (unit_two * gain_two.astype(jnp.float32)[None, :]).astype(jnp.bfloat16)
    gate_pre = jnp.dot(normed_two, gate_full, preferred_element_type=jnp.float32)
    up_pre = jnp.dot(normed_two, up_full, preferred_element_type=jnp.float32)
    sigmoid_gate = jax.nn.sigmoid(gate_pre)
    silu_gate = gate_pre * sigmoid_gate
    activation = (silu_gate * up_pre).astype(jnp.bfloat16)
    mlp_part = jnp.dot(activation, down_full, preferred_element_type=jnp.float32)
    block_output = (
        residual + lax.psum(mlp_part.astype(jnp.bfloat16), "tensor").astype(jnp.float32)
    ).astype(jnp.bfloat16)
    act_delta = jnp.dot(cotangent, down_full.T, preferred_element_type=jnp.float32)
    silu_slope = sigmoid_gate * (1.0 + gate_pre * (1.0 - sigmoid_gate))
    gate_delta = (act_delta * up_pre * silu_slope).astype(jnp.bfloat16)
    up_delta = (act_delta * silu_gate).astype(jnp.bfloat16)
    down_term = jnp.dot(activation.T, cotangent, preferred_element_type=jnp.float32)
    gate_term = jnp.dot(normed_two.T, gate_delta, preferred_element_type=jnp.float32)
    up_term = jnp.dot(normed_two.T, up_delta, preferred_element_type=jnp.float32)
    normed_two_part = jnp.dot(
        gate_delta, gate_full.T, preferred_element_type=jnp.float32
    ) + jnp.dot(up_delta, up_full.T, preferred_element_type=jnp.float32)
    normed_two_delta = lax.psum(normed_two_part, "tensor")
    gain_two_term, residual_back = norm_backward(normed_two_delta, unit_two, rstd_two, gain_two)
    residual_delta = cotangent.astype(jnp.float32) + residual_back
    residual_low = residual_delta.astype(jnp.bfloat16)
    output_term = jnp.dot(attended_rows.T, residual_low, preferred_element_type=jnp.float32)
    attended_delta = jnp.dot(
        residual_low, output_full.T, preferred_element_type=jnp.float32
    ).astype(jnp.bfloat16)
    delta_heads = jnp.moveaxis(attended_delta.reshape(row_count, kv_local, head_share, HD), 1, 0)
    inner_rows = jnp.moveaxis(
        jnp.sum(attended.astype(jnp.float32) * delta_heads.astype(jnp.float32), axis=-1), 2, 1
    )
    query_back, key_back, value_back = lax.map(
        lambda parts_h: head_backward(
            parts_h[0],
            parts_h[1],
            parts_h[2],
            parts_h[3],
            parts_h[4],
            parts_h[5],
            allowed,
            score_scale,
        ),
        (query_heads, key_heads, value_heads, log_total, delta_heads, inner_rows),
    )
    key_sum, value_sum = (
        lax.psum_scatter(
            jnp.moveaxis(key_back, 0, 1).reshape(group_rows, kv_local * HD).astype(jnp.bfloat16),
            "ctx",
            scatter_dimension=0,
            tiled=True,
        ).astype(jnp.float32),
        lax.psum_scatter(
            jnp.moveaxis(value_back, 0, 1).reshape(group_rows, kv_local * HD).astype(jnp.bfloat16),
            "ctx",
            scatter_dimension=0,
            tiled=True,
        ).astype(jnp.float32),
    )
    query_delta = rotate(
        jnp.moveaxis(query_back, 0, 1).reshape(row_count, heads_local, HD),
        cosine_table,
        sine_table,
        -1.0,
    )
    query_delta = query_delta.reshape(row_count, heads_local * HD).astype(jnp.bfloat16)
    key_delta = rotate(key_sum.reshape(row_count, kv_local, HD), cosine_table, sine_table, -1.0)
    key_delta = key_delta.reshape(row_count, kv_local * HD).astype(jnp.bfloat16)
    value_delta = value_sum.astype(jnp.bfloat16)
    query_term = jnp.dot(normed_one.T, query_delta, preferred_element_type=jnp.float32)
    key_term = jnp.dot(normed_one.T, key_delta, preferred_element_type=jnp.float32)
    value_term = jnp.dot(normed_one.T, value_delta, preferred_element_type=jnp.float32)
    normed_one_part = (
        jnp.dot(query_delta, query_full.T, preferred_element_type=jnp.float32)
        + jnp.dot(key_delta, key_full.T, preferred_element_type=jnp.float32)
        + jnp.dot(value_delta, value_full.T, preferred_element_type=jnp.float32)
    )
    normed_one_delta = lax.psum(normed_one_part.astype(jnp.bfloat16), "tensor").astype(jnp.float32)
    gain_one_term, input_back = norm_backward(normed_one_delta, unit_one, rstd_one, gain_one)
    input_grad = residual_delta + input_back
    gain_one_s, query_s, key_s, value_s, output_s, gain_two_s, gate_s, up_s, down_s = (
        lax.psum_scatter(
            gain_one_term.astype(jnp.bfloat16), "fsdp", scatter_dimension=0, tiled=True
        ).astype(jnp.float32),
        lax.psum_scatter(
            query_term.astype(jnp.bfloat16), "fsdp", scatter_dimension=0, tiled=True
        ).astype(jnp.float32),
        lax.psum_scatter(
            key_term.astype(jnp.bfloat16), "fsdp", scatter_dimension=0, tiled=True
        ).astype(jnp.float32),
        lax.psum_scatter(
            value_term.astype(jnp.bfloat16), "fsdp", scatter_dimension=0, tiled=True
        ).astype(jnp.float32),
        lax.psum_scatter(
            output_term.astype(jnp.bfloat16), "fsdp", scatter_dimension=1, tiled=True
        ).astype(jnp.float32),
        lax.psum_scatter(
            gain_two_term.astype(jnp.bfloat16), "fsdp", scatter_dimension=0, tiled=True
        ).astype(jnp.float32),
        lax.psum_scatter(
            gate_term.astype(jnp.bfloat16), "fsdp", scatter_dimension=0, tiled=True
        ).astype(jnp.float32),
        lax.psum_scatter(
            up_term.astype(jnp.bfloat16), "fsdp", scatter_dimension=0, tiled=True
        ).astype(jnp.float32),
        lax.psum_scatter(
            down_term.astype(jnp.bfloat16), "fsdp", scatter_dimension=1, tiled=True
        ).astype(jnp.float32),
    )
    gain_one_s, query_s, key_s, value_s, output_s, gain_two_s, gate_s, up_s, down_s = (
        lax.psum(gain_one_s.astype(jnp.bfloat16), "ctx").astype(jnp.float32),
        lax.psum(query_s.astype(jnp.bfloat16), "ctx").astype(jnp.float32),
        lax.psum(key_s.astype(jnp.bfloat16), "ctx").astype(jnp.float32),
        lax.psum(value_s.astype(jnp.bfloat16), "ctx").astype(jnp.float32),
        lax.psum(output_s.astype(jnp.bfloat16), "ctx").astype(jnp.float32),
        lax.psum(gain_two_s.astype(jnp.bfloat16), "ctx").astype(jnp.float32),
        lax.psum(gate_s.astype(jnp.bfloat16), "ctx").astype(jnp.float32),
        lax.psum(up_s.astype(jnp.bfloat16), "ctx").astype(jnp.float32),
        lax.psum(down_s.astype(jnp.bfloat16), "ctx").astype(jnp.float32),
    )
    return (
        block_output,
        input_grad,
        gain_one_s,
        query_s,
        key_s,
        value_s,
        output_s,
        gain_two_s,
        gate_s,
        up_s,
        down_s,
    )


def solution(mesh):
    in_specs = (
        P(("fsdp", "ctx"), None),
        P("fsdp", None),
        P("fsdp"),
        P("fsdp", "tensor"),
        P("fsdp", "tensor"),
        P("fsdp", "tensor"),
        P("tensor", "fsdp"),
        P("fsdp"),
        P("fsdp", "tensor"),
        P("fsdp", "tensor"),
        P("tensor", "fsdp"),
        P(("fsdp", "ctx"), None),
    )
    out_specs = (
        P(("fsdp", "ctx"), None),
        P(("fsdp", "ctx"), None),
        P("fsdp"),
        P("fsdp", "tensor"),
        P("fsdp", "tensor"),
        P("fsdp", "tensor"),
        P("tensor", "fsdp"),
        P("fsdp"),
        P("fsdp", "tensor"),
        P("fsdp", "tensor"),
        P("tensor", "fsdp"),
    )
    return jax.shard_map(body, mesh=mesh, in_specs=in_specs, out_specs=out_specs, check_vma=False)
```

profile of v0, /device:TPU:0, one launch (start us, length us, event | category | flops | bytes accessed | tf_op | source)
XLA Modules:
  0.0 1844.9 jit_solution(2427764517740190867)
XLA Ops:
  10.1 6.2 all-gather
  17.2 11.9 all-gather.10.cloned.1.call-done
  30.8 16.0 all_gather.35
  49.8 15.8 all_gather.37
  65.6 17.9 all-gather.14.cloned.1.call-done
  83.5 4.0 fusion.92
  87.7 16.2 while.28
  103.9 15.5 all-gather.16.cloned.1.call-done
  119.4 4.8 fusion.97
  126.4 5.4 all-gather.1
  131.8 55.6 %all-reduce.11.cloned.1.call-done = f32[256,2048]{1,0:T(8,128)} async-done(((f32[256,2048]{1,0:T(8,128)}), f32[256,2048]{1,0:T(8,128)}) %all-reduce.11.cloned.1.call-update) | async-done | bytes 2097168 | tf_op jit(solution)/shard_map/psum | solution.py:156
  190.5 104.2 %all-gather.18.cloned.1.call-done = bf16[2048,4096]{1,0:T(8,128)(2,1)} async-done(((bf16[512,4096]{1,0:T(8,128)(2,1)}), bf16[2048,4096]{1,0:T(8,128)(2,1)}) %all-gather.18.cloned.1.call-update) | async-done | bytes 16777232 | tf_op jit(solution)/shard_map/all_gather | solution.py:159
  294.7 12.9 fusion.98
  307.6 94.6 %all-gather.20.cloned.1.call-done = bf16[2048,4096]{1,0:T(8,128)(2,1)} async-done(((bf16[512,4096]{1,0:T(8,128)(2,1)}), bf16[2048,4096]{1,0:T(8,128)(2,1)}) %all-gather.20.cloned.1.call-update) | async-done | bytes 16777232 | tf_op jit(solution)/shard_map/all_gather | solution.py:160
  402.2 12.9 fusion.99
  415.1 94.5 %all-gather.22.cloned.1.call-done = bf16[4096,2048]{1,0:T(8,128)(2,1)} async-done(((bf16[4096,512]{1,0:T(8,128)(2,1)}), bf16[4096,2048]{1,0:T(8,128)(2,1)}) %all-gather.22.cloned.1.call-update) | async-done | bytes 16777232 | tf_op jit(solution)/shard_map/all_gather | solution.py:161
  509.7 13.6 multiply_convert_fusion
  523.2 12.2 fusion.100
  535.5 12.8 convolution_add_fusion.2
  548.6 62.9 %all-reduce.13.cloned.1.call-done = f32[256,2048]{1,0:T(8,128)} async-done(((f32[256,2048]{1,0:T(8,128)}), f32[256,2048]{1,0:T(8,128)}) %all-reduce.13.cloned.1.call-update) | async-done | bytes 2097168 | tf_op jit(solution)/shard_map/psum | solution.py:184
  622.4 40.6 %while.29 = (s32[]{:T(128)}, f32[4,256,4,64]{1,3,2,0:T(8,128)}, bf16[4,1024,64]{1,2,0:T(8,128)(2,1)}, bf16[4,1024,64]{1,2,0:T(8,128)(2,1)}, bf16[4,1024,64]{1,2,...) while((s32[]{:T(128)}, f32[4,256,4,64]{1,3,2,0:T(8,128)}, ...), condition=%wide.region_16.17_spmd.clone, body=%wide.region_15.16_spmd.clone.sunk | while | flops 683409408 | bytes 31890716 | solution.py:196
  624.5 2.4 fusion.176
  634.6 2.4 fusion.176
  644.8 2.4 fusion.176
  654.9 2.4 fusion.176
  663.8 21.2 %reduce-scatter.10.cloned.1.call-done = bf16[256,256]{0,1:T(8,128)(2,1)} async-done(((bf16[1024,256]{0,1:T(8,128)(2,1)}), bf16[256,256]{0,1:T(8,128)(2,1)}) %reduce-scatter.10.cloned.1.call-update) | async-done | bytes 131088 | tf_op jit(solution)/shard_map/reduce_scatter | solution.py:210
  687.7 19.7 %reduce-scatter.12.cloned.1.call-done = bf16[256,256]{0,1:T(8,128)(2,1)} async-done(((bf16[1024,256]{0,1:T(8,128)(2,1)}), bf16[256,256]{0,1:T(8,128)(2,1)}) %reduce-scatter.12.cloned.1.call-update) | async-done | bytes 131088 | tf_op jit(solution)/shard_map/reduce_scatter | solution.py:216
  707.4 2.5 convolution_convert_fusion.6
  712.2 3.4 convolution_convert_fusion.4
  715.7 5.1 convolution_convert_fusion.3
  721.1 12.2 convolution_convert_fusion.2
  733.4 12.6 convolution_convert_fusion.1
  746.3 12.1 convolution_convert_fusion
  758.5 12.1 convolution_convert_fusion.5
  775.0 32.7 %reduce-scatter.14.cloned.1.call-done = bf16[512,1024]{1,0:T(8,128)(2,1)} async-done(((bf16[2048,1024]{1,0:T(8,128)(2,1)}), bf16[512,1024]{1,0:T(8,128)(2,1)}) %reduce-scatter.14.cloned.1.call-update) | async-done | bytes 1048592 | tf_op jit(solution)/shard_map/reduce_scatter | solution.py:248
  807.8 47.4 %reduce-scatter.20.cloned.1.call-done = bf16[1024,512]{1,0:T(8,128)(2,1)} async-done(((bf16[1024,2048]{1,0:T(8,128)(2,1)}), bf16[1024,512]{1,0:T(8,128)(2,1)}) %reduce-scatter.20.cloned.1.call-update) | async-done | bytes 1048592 | tf_op jit(solution)/shard_map/reduce_scatter | solution.py:257
  855.2 127.5 %reduce-scatter.22.cloned.1.call-done = bf16[512,4096]{1,0:T(8,128)(2,1)} async-done(((bf16[2048,4096]{1,0:T(8,128)(2,1)}), bf16[512,4096]{1,0:T(8,128)(2,1)}) %reduce-scatter.22.cloned.1.call-update) | async-done | bytes 4194320 | tf_op jit(solution)/shard_map/reduce_scatter | solution.py:263
  982.7 127.5 %reduce-scatter.24.cloned.1.call-done = bf16[512,4096]{1,0:T(8,128)(2,1)} async-done(((bf16[2048,4096]{1,0:T(8,128)(2,1)}), bf16[512,4096]{1,0:T(8,128)(2,1)}) %reduce-scatter.24.cloned.1.call-update) | async-done | bytes 4194320 | tf_op jit(solution)/shard_map/reduce_scatter | solution.py:266
  1110.2 127.3 %reduce-scatter.26.cloned.1.call-done = bf16[4096,512]{1,0:T(8,128)(2,1)} async-done(((bf16[4096,2048]{1,0:T(8,128)(2,1)}), bf16[4096,512]{1,0:T(8,128)(2,1)}) %reduce-scatter.26.cloned.1.call-update) | async-done | bytes 4194320 | tf_op jit(solution)/shard_map/reduce_scatter | solution.py:269
  1239.4 64.0 %all-reduce.17.cloned.1.call-done = (bf16[256,2048]{1,0:T(8,128)(2,1)}, bf16[256,2048]{1,0:T(8,128)(2,1)}) async-done(((bf16[256,2048]{1,0:T(8,128)(2,1)}, bf16[256,2048]{1,0:T(8,128)(2,1)}), (bf16[256,2048]{1,0:T(8,128)(2,1)}, bf16[256,2048]{1,0:T(8,128)(2,1)})) %all-reduce.17.cloned.1.call-update) | async-done | bytes 2097168 | tf_op jit(solution)/shard_map/psum | solution.py:172
  1305.5 6.5 all-reduce.4
  1312.2 12.6 all-reduce.2
  1325.9 4.9 fusion.80
  1330.8 486.9 %all-reduce.15.cloned.1.call-done = (bf16[512,1024]{1,0:T(8,128)(2,1)}, bf16[512,256]{1,0:T(8,128)(2,1)}, bf16[512,256]{1,0:T(8,128)(2,1)}, bf16[1024,512]{1,0:T...) async-done(((bf16[512,1024]{1,0:T(8,128)(2,1)}, bf16[512,256]{1,0:T(8,128)(2,1)}, bf16[512,256]{1,0:T(8,128)(2,1)}, ...) | async-done | bytes 15204368 | tf_op jit(solution)/shard_map/psum | solution.py:275
  1817.8 2.9 convert_element_type.229
  1824.0 4.5 convert_element_type.239
  1828.5 4.5 convert_element_type.241
  1833.0 4.6 convert_element_type.243
  (228 shorter events, 90.4 us)
Async XLA Ops:
  7.2 2.9 copy-start.23
  7.2 9.1 copy-start
  7.2 9.4 copy-start.25
  7.2 21.9 %all-gather.10.cloned.1.call-start = ((), (), s32[]{:S(2)}) async-start(), calls=%async_computation.9 | async-start | bytes 1310720 | tf_op jit(solution)/shard_map/all_gather | solution.py:115
  7.9 39.9 %all-gather.12.cloned.1.call-start = ((), (), s32[]{:S(2)}) async-start(), calls=%async_computation.10 | async-start | bytes 1310720 | tf_op jit(solution)/shard_map/all_gather | solution.py:114
  8.7 74.8 %all-gather.14.cloned.1.call-start = ((), (), s32[]{:S(2)}) async-start(), calls=%async_computation.11 | async-start | bytes 5242880 | tf_op jit(solution)/shard_map/all_gather | solution.py:113
  9.4 110.0 %all-gather.16.cloned.1.call-start = ((), (), s32[]{:S(2)}) async-start(), calls=%async_computation.12 | async-start | bytes 5242880 | tf_op jit(solution)/shard_map/all_gather | solution.py:116
  10.0 177.3 %all-reduce.11.cloned.1.call-start = ((), (), s32[]{:S(2)}) async-start(), calls=%async_computation.13 | async-start | bytes 4194304 | tf_op jit(solution)/shard_map/psum | solution.py:156
  103.9 20.3 %copy-start.3 = (bf16[4,1024,64]{1,2,0:T(8,128)(2,1)}, bf16[4,1024,64]{1,2,0:T(8,128)(2,1)S(1)}, u32[]{:S(2)}) copy-start(bf16[4,1024,64]{1,2,0:T(8,128)(2,1)S(1)} %get-tuple-element.519) | copy-start | bytes 1572868
  103.9 20.3 %copy-start.4 = (bf16[4,256,4,64]{1,3,2,0:T(8,128)(2,1)}, bf16[4,256,4,64]{1,3,2,0:T(8,128)(2,1)S(1)}, u32[]{:S(2)}) copy-start(bf16[4,256,4,64]{1,3,2,0:T(8,128)(2,1)S(1)} %get-tuple-element.520) | copy-start | bytes 1572868
  103.9 20.3 %copy-start.9 = (bf16[4,256,4,64]{1,3,2,0:T(8,128)(2,1)}, bf16[4,256,4,64]{1,3,2,0:T(8,128)(2,1)S(1)}, u32[]{:S(2)}) copy-start(bf16[4,256,4,64]{1,3,2,0:T(8,128)(2,1)S(1)} %get-tuple-element.108) | copy-start | bytes 1572868
  124.2 170.5 %all-gather.18.cloned.1.call-start = ((), (), s32[]{:S(2)}) async-start(), calls=%async_computation.14 | async-start | bytes 20971520 | tf_op jit(solution)/shard_map/all_gather | solution.py:159
  124.8 277.4 %all-gather.20.cloned.1.call-start = ((), (), s32[]{:S(2)}) async-start(), calls=%async_computation.15 | async-start | bytes 20971520 | tf_op jit(solution)/shard_map/all_gather | solution.py:160
  125.5 384.1 %all-gather.22.cloned.1.call-start = ((), (), s32[]{:S(2)}) async-start(), calls=%async_computation.16 | async-start | bytes 20971520 | tf_op jit(solution)/shard_map/all_gather | solution.py:161
  126.3 485.1 %all-reduce.13.cloned.1.call-start = ((), (), s32[]{:S(2)}) async-start(), calls=%async_computation.17 | async-start | bytes 4194304 | tf_op jit(solution)/shard_map/psum | solution.py:184
  548.3 136.7 %reduce-scatter.10.cloned.1.call-start = ((), (), s32[]{:S(2)}) async-start(), calls=%async_computation.18 | async-start | bytes 655360 | tf_op jit(solution)/shard_map/reduce_scatter | solution.py:210
  611.4 2.3 copy-start.2
  611.4 2.5 copy-start.8
  613.9 2.9 copy-start.27
  622.4 2.1 copy-start.12
  626.9 2.2 copy-start.16
  626.9 3.9 copy-start.18
  632.6 2.0 copy-start.12
  637.0 2.2 copy-start.16
  637.0 3.9 copy-start.18
  642.7 2.0 copy-start.12
  647.2 2.2 copy-start.16
  647.2 3.9 copy-start.18
  657.3 2.2 copy-start.16
  657.3 3.9 copy-start.18
  663.0 44.4 %reduce-scatter.12.cloned.1.call-start = ((), (), s32[]{:S(2)}) async-start(), calls=%async_computation.19 | async-start | bytes 655360 | tf_op jit(solution)/shard_map/reduce_scatter | solution.py:216
  663.8 111.2 %reduce-scatter.16.cloned.1.call-start = ((), (), s32[]{:S(2)}) async-start(), calls=%async_computation.21 | async-start | bytes 1310720 | tf_op jit(solution)/shard_map/reduce_scatter | solution.py:251
  687.7 87.4 %reduce-scatter.18.cloned.1.call-start = ((), (), s32[]{:S(2)}) async-start(), calls=%async_computation.22 | async-start | bytes 1310720 | tf_op jit(solution)/shard_map/reduce_scatter | solution.py:254
  709.9 97.9 %reduce-scatter.14.cloned.1.call-start = ((), (), s32[]{:S(2)}) async-start(), calls=%async_computation.20 | async-start | bytes 5242880 | tf_op jit(solution)/shard_map/reduce_scatter | solution.py:248
  715.6 139.5 %reduce-scatter.20.cloned.1.call-start = ((), (), s32[]{:S(2)}) async-start(), calls=%async_computation.23 | async-start | bytes 5242880 | tf_op jit(solution)/shard_map/reduce_scatter | solution.py:257
  720.8 261.9 %reduce-scatter.22.cloned.1.call-start = ((), (), s32[]{:S(2)}) async-start(), calls=%async_computation.24 | async-start | bytes 20971520 | tf_op jit(solution)/shard_map/reduce_scatter | solution.py:263
  733.3 376.8 %reduce-scatter.24.cloned.1.call-start = ((), (), s32[]{:S(2)}) async-start(), calls=%async_computation.25 | async-start | bytes 20971520 | tf_op jit(solution)/shard_map/reduce_scatter | solution.py:266
  746.0 491.5 %reduce-scatter.26.cloned.1.call-start = ((), (), s32[]{:S(2)}) async-start(), calls=%async_computation.26 | async-start | bytes 20971520 | tf_op jit(solution)/shard_map/reduce_scatter | solution.py:269
  758.5 545.0 %all-reduce.17.cloned.1.call-start = ((), (), s32[]{:S(2)}) async-start(), calls=%async_computation.28 | async-start | bytes 4194304 | tf_op jit(solution)/shard_map/psum | solution.py:172
  758.5 12.1 copy-start.11
  758.5 12.1 copy-start.26
  774.9 1042.8 %all-reduce.15.cloned.1.call-start = ((), (), s32[]{:S(2)}) async-start(), calls=%async_computation.27 | async-start | bytes 30408704 | tf_op jit(solution)/shard_map/psum | solution.py:275
  1817.8 2.9 copy-start.21
  1817.8 3.7 copy-start.20
  1817.8 4.6 copy-start.13
  1820.7 3.3 copy-start.7
  1824.0 4.5 copy-start.6
  1828.5 4.5 copy-start.5
  (16 other events, 17.1 us)
Sparse Core Ops, SparseCore 0:
  9.6 19.4 all-gather.9
  30.6 16.7 all-gather.11
  49.0 34.4 all-gather.13
  84.9 34.4 all-gather.15
  124.3 62.9 all-reduce.10
  188.8 105.8 all-gather.17
  296.2 105.8 all-gather.19
  403.7 105.8 all-gather.21
  548.4 62.9 all-reduce.12
  663.2 21.8 reduce-scatter.9
  687.3 20.0 reduce-scatter.11
  709.8 22.9 reduce-scatter.15
  735.4 24.8 reduce-scatter.17
  763.2 44.5 reduce-scatter.13
  810.7 44.3 reduce-scatter.19
  857.6 125.0 reduce-scatter.21
  985.1 125.0 reduce-scatter.23
  1112.6 124.8 reduce-scatter.25
  1240.5 62.9 all-reduce.16
  1306.8 510.9 all-reduce.14
where the time goes:
time: 1850 us; the launch traced here: 1840 us
  waiting for transfers between devices  1520 us (82%)
  matrix products  191 us (10%)
  blocking collectives  62.5 us (3%)
  other arithmetic  45.1 us (2%)
    psum x1, waiting for transfers between devices, body(): lax.psum(query_s.astype(jnp.bfloat16), 'ctx').astype(jnp.float32)  487 us
    reduce_scatter x1, waiting for transfers between devices, body(): lax.psum_scatter(gate_term.astype(jnp.bfloat16), 'fsdp', scatter_dimensio...  128 us
    reduce_scatter x1, waiting for transfers between devices, body(): lax.psum_scatter(up_term.astype(jnp.bfloat16), 'fsdp', scatter_dimension=...  128 us
    reduce_scatter x1, waiting for transfers between devices, body(): lax.psum_scatter(down_term.astype(jnp.bfloat16), 'fsdp', scatter_dimensio...  127 us
    all_gather x1, waiting for transfers between devices, body(): lax.all_gather(w_gate, 'fsdp', axis=0, tiled=True)  104 us
    all_gather x1, waiting for transfers between devices, body(): lax.all_gather(w_up, 'fsdp', axis=0, tiled=True)  94.6 us
    all_gather x1, waiting for transfers between devices, body(): lax.all_gather(w_down, 'fsdp', axis=1, tiled=True)  94.5 us
    psum x1, waiting for transfers between devices, body(): lax.psum(mlp_part.astype(jnp.bfloat16), 'tensor').astype(jnp.float32)  64 us
  transfers between devices with their start and end apart: 20, of which 17 were waited for; matrix products, arithmetic and copies ran while one was open for 7% of the time, Pallas kernels for 0%

commit v1 on v0

--- a/solution.py
+++ b/solution.py
@@ -7,6 +7,17 @@
 HD = 64
 eps_norm = 1e-05
 rope_base = 500000.0
+
+
+def ring_gather(array, axis, dim):
+    ways = lax.axis_size(axis)
+    pieces = [array]
+    for far in range(1, ways):
+        pieces.append(
+            lax.ppermute(pieces[far - 1], axis, [(d, (d - 1) % ways) for d in range(ways)])
+        )
+    line = jnp.concatenate(pieces, axis=dim)
+    return jnp.roll(line, lax.axis_index(axis) * array.shape[dim], axis=dim)
 
 
 def layout(lengths_row, token_index):
@@ -156,7 +167,7 @@
     residual = input_wide + lax.psum(attn_part, "tensor")
     gain_two, gate_full, up_full, down_full = (
         lax.all_gather(mlp_gain, "fsdp", axis=0, tiled=True),
-        lax.all_gather(w_gate, "fsdp", axis=0, tiled=True),
+        ring_gather(w_gate, "fsdp", 0),
         lax.all_gather(w_up, "fsdp", axis=0, tiled=True),
         lax.all_gather(w_down, "fsdp", axis=1, tiled=True),
     )

time: 1850 us -> 1810 us (0.978)
  waiting for transfers between devices: 1520 us -> 1330 us
  blocking collectives: 62.5 us -> 161 us
  local copies, waits for them, and re-layouts: 12.1 us -> 46.6 us
    ppermute x0 -> x3, waiting for transfers between devices: none -> 136 us  [ring_gather(): lax.ppermute(pieces[far - 1], axis, [(d, (d - 1) % ways) for d in range(w...]
    all_gather x1 -> x0, waiting for transfers between devices: 104 us -> none  [body(): lax.all_gather(w_gate, 'fsdp', axis=0, tiled=True)]
    all_gather x1, blocking collectives: 5.4 us -> 104 us  [body(): lax.all_gather(mlp_gain, 'fsdp', axis=0, tiled=True)]
    all_gather x1, waiting for transfers between devices: 94.6 us -> 0.01 us  [body(): lax.all_gather(w_up, 'fsdp', axis=0, tiled=True)]
    all_gather x1, waiting for transfers between devices: 94.5 us -> 31.2 us  [body(): lax.all_gather(w_down, 'fsdp', axis=1, tiled=True)]
    psum x1, waiting for transfers between devices: 55.6 us -> 0.01 us  [body(): residual = input_wide + lax.psum(attn_part, 'tensor')]
    unnamed x53 -> x64, local copies, waits for them, and re-layouts: 5.75 us -> 35.6 us
  transfers between devices with their start and end apart: 20 -> 22, of which waited for: 17 -> 16; matrix products, arithmetic and copies ran while one was open for 7% -> 8% of each run, Pallas kernels for 0% -> 0%
where the time goes in v1:
time: 1810 us; the launch traced here: 1800 us
  waiting for transfers between devices  1330 us (73%)
  matrix products  193 us (11%)
  blocking collectives  161 us (9%)
  other arithmetic  48.7 us (3%)
  local copies, waits for them, and re-layouts  46.6 us (3%)
    psum x1, waiting for transfers between devices, body(): lax.psum(query_s.astype(jnp.bfloat16), 'ctx').astype(jnp.float32)  487 us
    ppermute x3, waiting for transfers between devices, ring_gather(): lax.ppermute(pieces[far - 1], axis, [(d, (d - 1) % ways) for d in range(w...  136 us
    reduce_scatter x1, waiting for transfers between devices, body(): lax.psum_scatter(up_term.astype(jnp.bfloat16), 'fsdp', scatter_dimension=...  128 us
    reduce_scatter x1, waiting for transfers between devices, body(): lax.psum_scatter(gate_term.astype(jnp.bfloat16), 'fsdp', scatter_dimensio...  128 us
    reduce_scatter x1, waiting for transfers between devices, body(): lax.psum_scatter(down_term.astype(jnp.bfloat16), 'fsdp', scatter_dimensio...  127 us
    all_gather x1, blocking collectives, body(): lax.all_gather(mlp_gain, 'fsdp', axis=0, tiled=True)  104 us
    psum x1, waiting for transfers between devices, body(): lax.psum(mlp_part.astype(jnp.bfloat16), 'tensor').astype(jnp.float32)  63.9 us
    psum x1, waiting for transfers between devices, body(): normed_two_delta = lax.psum(normed_two_part, 'tensor')  62.9 us
  transfers between devices with their start and end apart: 22, of which 16 were waited for; matrix products, arithmetic and copies ran while one was open for 8% of the time, Pallas kernels for 0%

profile of v1, /device:TPU:0, one launch (start us, length us, event | category | flops | bytes accessed | tf_op | source)
XLA Modules:
  0.0 1803.2 jit_solution(10201216505903942282)
XLA Ops:
  12.4 6.2 all-gather
  20.3 8.7 all-gather.11.cloned.1.call-done
  31.3 16.0 all_gather.34
  49.0 16.0 all_gather.32
  66.1 17.3 all-gather.13.cloned.1.call-done
  83.4 4.0 fusion.101
  87.6 16.2 while.28
  103.8 15.5 all-gather.15.cloned.1.call-done
  119.3 4.8 fusion.106
  125.7 46.3 %collective-permute-done = bf16[512,4096]{1,0:T(8,128)(2,1)S(1)} collective-permute-done((bf16[512,4096]{1,0:T(8,128)(2,1)}, bf16[512,4096]{1,0:T(8,128)(2,1)S(1)}, u32[]{:S(2)}, u32[]{:S(2)}) %collective-permute-start) | collective-permute-done | bytes 4194336 | tf_op jit(solution)/shard_map/ppermute | solution.py:17
  176.3 89.9 %collective-permute-done.1 = bf16[512,4096]{1,0:T(8,128)(2,1)} collective-permute-done((bf16[512,4096]{1,0:T(8,128)(2,1)S(1)}, bf16[512,4096]{1,0:T(8,128)(2,1)}, u32[]{:S(2)}, u32[]{:S(2)}) %collective-permute-start.1) | collective-permute-done | bytes 4194336 | tf_op jit(solution)/shard_map/ppermute | solution.py:17
  268.5 103.8 %all-gather.1 = bf16[4,1,512]{2,1,0:T(2,128)(2,1)S(1)} all-gather(bf16[1,1,512]{2,1,0:T(2,128)(2,1)S(1)} %reshape.251), channel_id=1, replica_groups=mesh['fsdp'=4,'ctx'=4,'tensor'=2] {'fsdp'}, dimensions={0}, use_global_device_ids=true | all-gather | bytes 5120 | tf_op jit(solution)/shard_map/all_gather | solution.py:169
  372.3 4.8 constant_dynamic-update-slice_fusion.7
  382.6 4.8 constant_dynamic-update-slice_fusion.5
  387.4 4.8 constant_dynamic-update-slice_fusion.4
  398.2 4.7 constant_dynamic-update-slice_fusion.1
  402.8 4.6 constant_dynamic-update-slice_fusion
  407.5 12.6 fusion.107
  420.1 31.2 %all-gather.19.cloned.1.call-done = bf16[4096,2048]{1,0:T(8,128)(2,1)} async-done(((bf16[4096,512]{1,0:T(8,128)(2,1)}), bf16[4096,2048]{1,0:T(8,128)(2,1)}) %all-gather.19.cloned.1.call-update) | async-done | bytes 16777232 | tf_op jit(solution)/shard_map/all_gather | solution.py:172
  451.3 12.6 fusion.108
  464.0 13.9 multiply_convert_fusion.1
  477.9 12.2 fusion.109
  490.1 12.8 fusion.81
  503.2 62.9 %all-reduce.13.cloned.1.call-done = f32[256,2048]{1,0:T(8,128)} async-done(((f32[256,2048]{1,0:T(8,128)}), f32[256,2048]{1,0:T(8,128)}) %all-reduce.13.cloned.1.call-update) | async-done | bytes 2097168 | tf_op jit(solution)/shard_map/psum | solution.py:195
  576.9 43.0 %while.29 = (s32[]{:T(128)}, f32[4,256,4,64]{1,3,2,0:T(8,128)}, bf16[4,1024,64]{1,2,0:T(8,128)(2,1)}, bf16[4,1024,64]{1,2,0:T(8,128)(2,1)}, bf16[4,1024,64]{1,2,...) while((s32[]{:T(128)}, f32[4,256,4,64]{1,3,2,0:T(8,128)}, ...), condition=%wide.region_16.17_spmd.clone, body=%wide.region_15.16_spmd.clone.sunk | while | flops 683409408 | bytes 27696348 | solution.py:207
  579.0 2.5 fusion.183
  611.2 2.5 fusion.183
  620.5 21.4 %reduce-scatter.10.cloned.1.call-done = bf16[256,256]{0,1:T(8,128)(2,1)} async-done(((bf16[1024,256]{0,1:T(8,128)(2,1)}), bf16[256,256]{0,1:T(8,128)(2,1)}) %reduce-scatter.10.cloned.1.call-update) | async-done | bytes 131088 | tf_op jit(solution)/shard_map/reduce_scatter | solution.py:221
  644.6 20.2 %reduce-scatter.12.cloned.1.call-done = bf16[256,256]{0,1:T(8,128)(2,1)} async-done(((bf16[1024,256]{0,1:T(8,128)(2,1)}), bf16[256,256]{0,1:T(8,128)(2,1)}) %reduce-scatter.12.cloned.1.call-update) | async-done | bytes 131088 | tf_op jit(solution)/shard_map/reduce_scatter | solution.py:227
  667.3 5.0 convolution_convert_fusion.3
  674.7 3.4 convolution_convert_fusion.4
  678.4 12.2 convolution_convert_fusion.2
  690.7 12.6 convolution_convert_fusion.1
  703.6 12.1 convolution_convert_fusion
  715.8 12.1 convolution_convert_fusion.5
  732.4 32.8 %reduce-scatter.20.cloned.1.call-done = bf16[1024,512]{1,0:T(8,128)(2,1)} async-done(((bf16[1024,2048]{1,0:T(8,128)(2,1)}), bf16[1024,512]{1,0:T(8,128)(2,1)}) %reduce-scatter.20.cloned.1.call-update) | async-done | bytes 1048592 | tf_op jit(solution)/shard_map/reduce_scatter | solution.py:268
  765.2 47.6 %reduce-scatter.14.cloned.1.call-done = bf16[512,1024]{1,0:T(8,128)(2,1)} async-done(((bf16[2048,1024]{1,0:T(8,128)(2,1)}), bf16[512,1024]{1,0:T(8,128)(2,1)}) %reduce-scatter.14.cloned.1.call-update) | async-done | bytes 1048592 | tf_op jit(solution)/shard_map/reduce_scatter | solution.py:259
  812.8 127.5 %reduce-scatter.22.cloned.1.call-done = bf16[512,4096]{1,0:T(8,128)(2,1)} async-done(((bf16[2048,4096]{1,0:T(8,128)(2,1)}), bf16[512,4096]{1,0:T(8,128)(2,1)}) %reduce-scatter.22.cloned.1.call-update) | async-done | bytes 4194320 | tf_op jit(solution)/shard_map/reduce_scatter | solution.py:274
  940.3 127.5 %reduce-scatter.24.cloned.1.call-done = bf16[512,4096]{1,0:T(8,128)(2,1)} async-done(((bf16[2048,4096]{1,0:T(8,128)(2,1)}), bf16[512,4096]{1,0:T(8,128)(2,1)}) %reduce-scatter.24.cloned.1.call-update) | async-done | bytes 4194320 | tf_op jit(solution)/shard_map/reduce_scatter | solution.py:277
  1067.8 127.3 %reduce-scatter.26.cloned.1.call-done = bf16[4096,512]{1,0:T(8,128)(2,1)} async-done(((bf16[4096,2048]{1,0:T(8,128)(2,1)}), bf16[4096,512]{1,0:T(8,128)(2,1)}) %reduce-scatter.26.cloned.1.call-update) | async-done | bytes 4194320 | tf_op jit(solution)/shard_map/reduce_scatter | solution.py:280
  1197.0 63.9 %all-reduce.17.cloned.1.call-done = (bf16[256,2048]{1,0:T(8,128)(2,1)}, bf16[256,2048]{1,0:T(8,128)(2,1)}) async-done(((bf16[256,2048]{1,0:T(8,128)(2,1)}, bf16[256,2048]{1,0:T(8,128)(2,1)}), (bf16[256,2048]{1,0:T(8,128)(2,1)}, bf16[256,2048]{1,0:T(8,128)(2,1)})) %all-reduce.17.cloned.1.call-update) | async-done | bytes 2097168 | tf_op jit(solution)/shard_map/psum | solution.py:183
  1262.9 6.5 all-reduce.4
  1269.6 12.6 all-reduce.2
  1283.3 4.9 fusion.87
  1288.2 487.1 %all-reduce.15.cloned.1.call-done = (bf16[512,1024]{1,0:T(8,128)(2,1)}, bf16[512,256]{1,0:T(8,128)(2,1)}, bf16[512,256]{1,0:T(8,128)(2,1)}, bf16[1024,512]{1,0:T...) async-done(((bf16[512,1024]{1,0:T(8,128)(2,1)}, bf16[512,256]{1,0:T(8,128)(2,1)}, bf16[512,256]{1,0:T(8,128)(2,1)}, ...) | async-done | bytes 15204368 | tf_op jit(solution)/shard_map/psum | solution.py:286
  1775.4 6.8 convert_element_type.239
  1782.2 4.5 convert_element_type.241
  1786.7 4.6 convert_element_type.243
  (227 shorter events, 119.3 us)
Async XLA Ops:
  7.2 40.1 %copy-start = (bf16[256,2048]{1,0:T(8,128)(2,1)S(1)}, bf16[256,2048]{1,0:T(8,128)(2,1)}, u32[]{:S(2)}) copy-start(bf16[256,2048]{1,0:T(8,128)(2,1)} %param.16) | copy-start | bytes 3145732
  7.2 21.8 %all-gather.11.cloned.1.call-start = ((), (), s32[]{:S(2)}) async-start(), calls=%async_computation.10 | async-start | bytes 1310720 | tf_op jit(solution)/shard_map/all_gather | solution.py:125
  7.9 39.4 %all-gather.9.cloned.1.call-start = ((), (), s32[]{:S(2)}) async-start(), calls=%async_computation.9 | async-start | bytes 1310720 | tf_op jit(solution)/shard_map/all_gather | solution.py:126
  8.7 74.7 %all-gather.13.cloned.1.call-start = ((), (), s32[]{:S(2)}) async-start(), calls=%async_computation.11 | async-start | bytes 5242880 | tf_op jit(solution)/shard_map/all_gather | solution.py:124
  9.4 109.9 %all-gather.15.cloned.1.call-start = ((), (), s32[]{:S(2)}) async-start(), calls=%async_computation.12 | async-start | bytes 5242880 | tf_op jit(solution)/shard_map/all_gather | solution.py:127
  10.0 369.4 %all-reduce.11.cloned.1.call-start = ((), (), s32[]{:S(2)}) async-start(), calls=%async_computation.13 | async-start | bytes 4194304 | tf_op jit(solution)/shard_map/psum | solution.py:167
  103.8 20.3 %copy-start.7 = (bf16[4,1024,64]{1,2,0:T(8,128)(2,1)}, bf16[4,1024,64]{1,2,0:T(8,128)(2,1)S(1)}, u32[]{:S(2)}) copy-start(bf16[4,1024,64]{1,2,0:T(8,128)(2,1)S(1)} %get-tuple-element.521) | copy-start | bytes 1572868
  103.8 20.3 %copy-start.8 = (bf16[4,256,4,64]{1,3,2,0:T(8,128)(2,1)}, bf16[4,256,4,64]{1,3,2,0:T(8,128)(2,1)S(1)}, u32[]{:S(2)}) copy-start(bf16[4,256,4,64]{1,3,2,0:T(8,128)(2,1)S(1)} %get-tuple-element.522) | copy-start | bytes 1572868
  103.8 20.3 %copy-start.12 = (bf16[4,256,4,64]{1,3,2,0:T(8,128)(2,1)}, bf16[4,256,4,64]{1,3,2,0:T(8,128)(2,1)S(1)}, u32[]{:S(2)}) copy-start(bf16[4,256,4,64]{1,3,2,0:T(8,128)(2,1)S(1)} %get-tuple-element.108) | copy-start | bytes 1572868
  124.1 144.4 %copy-start.25 = (bf16[512]{0:T(512)(128)(2,1)S(1)}, bf16[512]{0:T(512)(128)(2,1)}, u32[]{:S(2)}) copy-start(bf16[512]{0:T(512)(128)(2,1)} %param.23) | copy-start | bytes 3076
  124.1 283.4 %all-gather.17.cloned.1.call-start = ((), (), s32[]{:S(2)}) async-start(), calls=%async_computation.14 | async-start | bytes 20971520 | tf_op jit(solution)/shard_map/all_gather | solution.py:171
  124.7 326.7 %all-gather.19.cloned.1.call-start = ((), (), s32[]{:S(2)}) async-start(), calls=%async_computation.15 | async-start | bytes 20971520 | tf_op jit(solution)/shard_map/all_gather | solution.py:172
  125.4 440.7 %all-reduce.13.cloned.1.call-start = ((), (), s32[]{:S(2)}) async-start(), calls=%async_computation.16 | async-start | bytes 4194304 | tf_op jit(solution)/shard_map/psum | solution.py:195
  125.5 46.6 %collective-permute-start = (bf16[512,4096]{1,0:T(8,128)(2,1)}, bf16[512,4096]{1,0:T(8,128)(2,1)S(1)}, u32[]{:S(2)}, u32[]{:S(2)}) collective-permute-start(bf16[512,4096]{1,0:T(8,128)(2,1)} %param.24), channel_id=1, source_target_pairs={{0,24},{8,0},{16,8},{24,16},{1,25},{9,1},{17,9},{25,17},{2,26},{10... | collective-permute-start | bytes 12582920 | tf_op jit(solution)/shard_map/ppermute | solution.py:17
  174.1 92.1 %collective-permute-start.1 = (bf16[512,4096]{1,0:T(8,128)(2,1)S(1)}, bf16[512,4096]{1,0:T(8,128)(2,1)}, u32[]{:S(2)}, u32[]{:S(2)}) collective-permute-start(bf16[512,4096]{1,0:T(8,128)(2,1)S(1)} %collective-permute-done), channel_id=1, source_target_pairs={{0,24},{8,0},{16,8},{24,16},{1,25},{9,1},{17,9},{25,17},{2,26},{10... | collective-permute-start | bytes 12582920 | tf_op jit(solution)/shard_map/ppermute | solution.py:17
  266.2 121.2 %collective-permute-start.2 = (bf16[512,4096]{1,0:T(8,128)(2,1)}, bf16[512,4096]{1,0:T(8,128)(2,1)}, u32[]{:S(2)}, u32[]{:S(2)}) collective-permute-start(bf16[512,4096]{1,0:T(8,128)(2,1)} %collective-permute-done.1), channel_id=1, source_target_pairs={{0,24},{8,0},{16,8},{24,16},{1,25},{9,1},{17,9},{25,17},{2,26},{10... | collective-permute-start | bytes 12582920 | tf_op jit(solution)/shard_map/ppermute | solution.py:17
  372.3 4.8 copy-start.4
  387.4 4.8 copy-start.2
  392.2 3.7 copy-start.5
  503.0 138.9 %reduce-scatter.10.cloned.1.call-start = ((), (), s32[]{:S(2)}) async-start(), calls=%async_computation.17 | async-start | bytes 655360 | tf_op jit(solution)/shard_map/reduce_scatter | solution.py:221
  566.1 2.3 copy-start.6
  566.1 2.5 copy-start.11
  568.4 3.0 copy-start.27
  576.9 2.1 copy-start.15
  579.0 4.6 copy-start.20
  587.7 2.0 copy-start.15
  589.7 4.6 copy-start.20
  600.5 4.6 copy-start.20
  609.1 2.0 copy-start.15
  611.2 4.6 copy-start.20
  619.9 44.8 %reduce-scatter.12.cloned.1.call-start = ((), (), s32[]{:S(2)}) async-start(), calls=%async_computation.18 | async-start | bytes 655360 | tf_op jit(solution)/shard_map/reduce_scatter | solution.py:227
  620.5 111.9 %reduce-scatter.16.cloned.1.call-start = ((), (), s32[]{:S(2)}) async-start(), calls=%async_computation.20 | async-start | bytes 1310720 | tf_op jit(solution)/shard_map/reduce_scatter | solution.py:262
  644.5 87.8 %reduce-scatter.18.cloned.1.call-start = ((), (), s32[]{:S(2)}) async-start(), calls=%async_computation.21 | async-start | bytes 1310720 | tf_op jit(solution)/shard_map/reduce_scatter | solution.py:265
  667.2 97.9 %reduce-scatter.20.cloned.1.call-start = ((), (), s32[]{:S(2)}) async-start(), calls=%async_computation.22 | async-start | bytes 5242880 | tf_op jit(solution)/shard_map/reduce_scatter | solution.py:268
  672.4 140.4 %reduce-scatter.14.cloned.1.call-start = ((), (), s32[]{:S(2)}) async-start(), calls=%async_computation.19 | async-start | bytes 5242880 | tf_op jit(solution)/shard_map/reduce_scatter | solution.py:259
  678.1 262.1 %reduce-scatter.22.cloned.1.call-start = ((), (), s32[]{:S(2)}) async-start(), calls=%async_computation.23 | async-start | bytes 20971520 | tf_op jit(solution)/shard_map/reduce_scatter | solution.py:274
  690.6 377.1 %reduce-scatter.24.cloned.1.call-start = ((), (), s32[]{:S(2)}) async-start(), calls=%async_computation.24 | async-start | bytes 20971520 | tf_op jit(solution)/shard_map/reduce_scatter | solution.py:277
  703.3 491.8 %reduce-scatter.26.cloned.1.call-start = ((), (), s32[]{:S(2)}) async-start(), calls=%async_computation.25 | async-start | bytes 20971520 | tf_op jit(solution)/shard_map/reduce_scatter | solution.py:280
  715.8 545.1 %all-reduce.17.cloned.1.call-start = ((), (), s32[]{:S(2)}) async-start(), calls=%async_computation.27 | async-start | bytes 4194304 | tf_op jit(solution)/shard_map/psum | solution.py:183
  715.8 12.1 copy-start.14
  715.8 12.1 copy-start.26
  732.3 1043.1 %all-reduce.15.cloned.1.call-start = ((), (), s32[]{:S(2)}) async-start(), calls=%async_computation.26 | async-start | bytes 30408704 | tf_op jit(solution)/shard_map/psum | solution.py:286
  1775.4 6.8 copy-start.10
  1782.2 4.5 copy-start.9
  1786.7 4.6 copy-start.17
  1786.7 6.2 copy-start.16
  1791.3 3.2 copy-start.23
  1791.3 4.0 copy-start.22
  (12 other events, 14.2 us)
Sparse Core Ops, SparseCore 0:
  9.6 19.4 all-gather.10
  30.6 16.6 all-gather.8
  48.9 34.4 all-gather.12
  84.8 34.4 all-gather.14
  124.2 62.9 all-reduce.10
  188.6 149.1 all-gather.16
  339.3 111.9 all-gather.18
  503.1 62.9 all-reduce.12
  620.0 21.8 reduce-scatter.9
  644.6 20.1 reduce-scatter.11
  667.3 23.0 reduce-scatter.15
  692.8 24.7 reduce-scatter.17
  720.7 44.4 reduce-scatter.19
  768.1 44.5 reduce-scatter.13
  815.2 125.0 reduce-scatter.21
  942.7 125.0 reduce-scatter.23
  1070.2 124.8 reduce-scatter.25
  1197.9 62.9 all-reduce.16
  1264.3 510.9 all-reduce.14
